TPU v7x, 32 devices: a whole 2x2x4 slice. The times are simulated.
32 devices in a mesh: edge: 4 (over y, x), tile: 8 (over z, core).
Axes of the slice: x: 2, y: 2, z: 4, core: 2. Of those that a mesh axis runs over, the one named last changes fastest.
Arguments:
- features: bfloat16 [96, 48, 64, 128], P('edge', 'tile'), may hold values from -6 to 6
- hidden_state: bfloat16 [32, 48, 64, 128], P('edge', 'tile'), may hold values from -1 to 1
- edge_source: int32 [32], P('edge'), may hold values from 0 to 23
- edge_owner: int32 [32, 1], P('edge'), may hold values from 0 to 3; in each aligned block of 8 rows (0 to 7, 8 to 15, ...) at most 4 rows name the same one
- edge_target: int32 [32], P('edge'), may hold values from 0 to 23
- edge_counts: int32 [4], P('edge'), may hold values from 4 to 8, as said below
- corr_weight: bfloat16 [49, 128], replicated, may hold values from -0.875 to 0.875
- gate_weight: bfloat16 [3, 3, 256, 256], replicated, may hold values from -0.125 to 0.125
- candidate_weight: bfloat16 [3, 3, 256, 128], replicated, may hold values from -0.125 to 0.125
- jacobian_weight: bfloat16 [128, 24], replicated, may hold values from -0.5 to 0.5
- confidence_weight: bfloat16 [128, 2], replicated, may hold values from -3 to 3
Outputs:
- hidden_next: bfloat16 [32, 48, 64, 128], P('edge', 'tile')
- camera_hessian: float32 [576, 576], P('tile', 'edge')
- pose_diagonal: float32 [96, 36], P('edge')
Inputs may be any that keep to these rules, and one draw needn't show every extreme that they name: `edge_owner`: in the rows of one index of edge at most 4 edges name the same owner, a bound that some block reaches. `edge_counts`: edges past a device's count are unused; some index of edge uses all 8.
All inputs are finite; a program needn't handle non-finite values.
Results may differ from a plain program's by a relative error of at most 0.015.
Values may be sent and summed in bfloat16 or wider, within the bound.
A program may use at most 128 MiB of HBM per device.

v0:
```python
import jax
import jax.numpy as jnp
from jax import lax
from jax.sharding import PartitionSpec as P

MAPH = 48
MAPW = 64
WINDOW = 7


def padded_2(cells, sides, width):
    for axis, dim in sides:
        count = lax.axis_size(axis)
        ends = count - 1
        head = lax.slice_in_dim(cells, 0, width, axis=dim)
        tail = lax.slice_in_dim(cells, cells.shape[dim] - width, cells.shape[dim], axis=dim)
        cells = jnp.concatenate(
            [
                lax.ppermute(tail, axis, [(i, (i + 1) % count) for i in range(ends)]),
                cells,
                lax.ppermute(head, axis, [((i + 1) % count, i) for i in range(ends)]),
            ],
            axis=dim,
        )
    return cells


def pad_columns(values):
    return jnp.pad(values, ((0, 0), (0, 0), (1, 1), (0, 0)))


def convolve(padded, weight):
    row_count = padded.shape[1] - 2
    col_count = padded.shape[2] - 2
    running = jnp.zeros((padded.shape[0], row_count, col_count, weight.shape[-1]), jnp.float32)
    for row_step in range(3):
        for col_step in range(3):
            window = padded[:, row_step : row_step + row_count, col_step : col_step + col_count]
            running = running + jnp.einsum(
                "erwc,ck->erwk",
                window,
                weight[row_step, col_step],
                preferred_element_type=jnp.float32,
            )
    return running


def per_device(
    features,
    hidden_state,
    edge_source,
    edge_owner,
    edge_target,
    edge_counts,
    corr_weight,
    gate_weight,
    candidate_weight,
    jacobian_weight,
    confidence_weight,
):
    edge_total = hidden_state.shape[0]
    frame_total = features.shape[0]
    band_rows = features.shape[1]
    map_width = features.shape[2]
    hidden_width = hidden_state.shape[3]
    owner_count = lax.axis_size("edge")
    slot_depth = max(2, (2 * edge_total + owner_count - 1) // owner_count)
    my_index = lax.axis_index("edge")
    in_use = jnp.arange(edge_total) < edge_counts[0]
    owners = edge_owner[:, 0]
    owner_hits = (owners[:, None] == jnp.arange(owner_count)[None, :]).astype(jnp.int32)
    earlier = jnp.cumsum(owner_hits, axis=0) - owner_hits
    rank_within = jnp.sum(earlier * owner_hits, axis=1)
    slot_index = owners * slot_depth + rank_within
    slot_hits = (slot_index[:, None] == jnp.arange(owner_count * slot_depth)[None, :]).astype(
        jnp.int32
    )
    source_global = my_index * frame_total + edge_source
    target_global = owners * frame_total + edge_target
    send_target = jnp.sum(slot_hits * edge_target[:, None], axis=0).reshape(owner_count, slot_depth)
    send_source = jnp.sum(slot_hits * source_global[:, None], axis=0).reshape(
        owner_count, slot_depth
    )
    got_target, got_source = (
        lax.all_to_all(send_target, "edge", split_axis=0, concat_axis=0, tiled=True),
        lax.all_to_all(send_source, "edge", split_axis=0, concat_axis=0, tiled=True),
    )
    asked = jnp.take(features, got_target.reshape(-1), axis=0).reshape(
        (owner_count, slot_depth) + features.shape[1:]
    )
    returned = lax.all_to_all(asked, "edge", split_axis=0, concat_axis=0, tiled=True)
    target_maps = jnp.take(
        returned.reshape((owner_count * slot_depth,) + features.shape[1:]), slot_index, axis=0
    )
    radius = WINDOW // 2
    source_maps = jnp.take(features, edge_source, axis=0)
    target_rows = padded_2(target_maps, (("tile", 1),), radius)
    target_padded = jnp.pad(target_rows, ((0, 0), (0, 0), (radius, radius), (0, 0)))
    columns = []
    for row_shift in range(WINDOW):
        for col_shift in range(WINDOW):
            moved = target_padded[
                :, row_shift : row_shift + band_rows, col_shift : col_shift + map_width
            ]
            columns.append(
                jnp.einsum("erwh,erwh->erw", source_maps, moved, preferred_element_type=jnp.float32)
            )
    corr = (jnp.stack(columns, axis=-1) * features.shape[3] ** (-0.5)).astype(jnp.bfloat16)
    motion = jax.nn.relu(
        jnp.einsum("ercd,dk->erck", corr, corr_weight, preferred_element_type=jnp.float32)
    ).astype(jnp.bfloat16)
    stacked = jnp.concatenate([hidden_state, motion], axis=-1)
    state_float = hidden_state.astype(jnp.float32)
    extended = padded_2(stacked, (("tile", 1),), 1)
    gates = jax.nn.sigmoid(convolve(pad_columns(extended), gate_weight))
    update = gates[..., :hidden_width]
    reset_state = (gates[..., hidden_width:] * state_float).astype(jnp.bfloat16)
    mixed = jnp.concatenate([reset_state, motion], axis=-1)
    mixed_extended = padded_2(mixed, (("tile", 1),), 1)
    candidate = jnp.tanh(convolve(pad_columns(mixed_extended), candidate_weight))
    new_state = ((1.0 - update) * state_float + update * candidate).astype(jnp.bfloat16)
    hidden_next = jnp.where(in_use[:, None, None, None], new_state, hidden_state)
    pixel_total = band_rows * map_width
    jacobian = jnp.einsum(
        "erwh,hk->ekrw", new_state, jacobian_weight, preferred_element_type=jnp.float32
    ).reshape(edge_total, 2, 12, pixel_total)
    confidence = jax.nn.softplus(
        jnp.einsum(
            "erwh,hk->ekrw", new_state, confidence_weight, preferred_element_type=jnp.float32
        )
    ).reshape(edge_total, 2, 1, pixel_total)
    normal_blocks = jnp.einsum(
        "ekap,ekbp->eab", jacobian * confidence, jacobian, precision=lax.Precision.HIGHEST
    ) / (MAPH * MAPW)
    normal_blocks = normal_blocks * in_use.astype(jnp.float32)[:, None, None]
    outgoing = jnp.concatenate(
        [
            normal_blocks[:, 6:, 6:].reshape(edge_total, 36),
            normal_blocks[:, :6, 6:].reshape(edge_total, 36),
        ],
        axis=1,
    )
    slot_blocks = jnp.einsum(
        "es,eq->sq", slot_hits.astype(jnp.float32), outgoing, precision=lax.Precision.HIGHEST
    ).reshape(owner_count, slot_depth, 72)
    incoming = lax.all_to_all(slot_blocks, "edge", split_axis=0, concat_axis=0, tiled=True).reshape(
        owner_count * slot_depth, 72
    )
    flat_target = got_target.reshape(-1)
    flat_source = got_source.reshape(-1)
    row_frames = jnp.concatenate(
        [source_global, target_global, my_index * frame_total + flat_target, flat_source]
    )
    col_frames = jnp.concatenate([edge_source, edge_source, flat_target, flat_target])
    block_list = jnp.concatenate(
        [
            normal_blocks[:, :6, :6],
            normal_blocks[:, 6:, :6],
            incoming[:, :36].reshape(-1, 6, 6),
            incoming[:, 36:].reshape(-1, 6, 6),
        ],
        axis=0,
    )
    on_diagonal = (row_frames == my_index * frame_total + col_frames).astype(jnp.float32)
    col_hits = (col_frames[:, None] == jnp.arange(frame_total)[None, :]).astype(jnp.float32)
    diagonal_part = jnp.einsum(
        "if,iq->fq",
        col_hits * on_diagonal[:, None],
        block_list.reshape(-1, 36),
        precision=lax.Precision.HIGHEST,
    )
    apart_blocks = block_list * (1.0 - on_diagonal)[:, None, None]
    spread = (apart_blocks[:, :, None, :] * col_hits[:, None, :, None]).reshape(
        -1, 6, frame_total * 6
    )
    own_rows = frame_total * owner_count * 6 // lax.axis_size("tile")
    frame_span = own_rows * lax.axis_size("tile") // 6
    row_hits = (row_frames[:, None] == jnp.arange(frame_span)[None, :]).astype(jnp.float32)
    placed = jnp.einsum("ic,ixq->cxq", row_hits, spread, precision=lax.Precision.HIGHEST)
    camera_hessian = lax.psum_scatter(
        placed.reshape(own_rows * lax.axis_size("tile"), frame_total * 6).astype(jnp.bfloat16),
        "tile",
        scatter_dimension=0,
        tiled=True,
    ).astype(jnp.float32)
    pose_diagonal = lax.psum(diagonal_part, "tile")
    return (hidden_next, camera_hessian, pose_diagonal)


def solution(mesh):
    placed = (
        P("edge", "tile", None, None),
        P("edge", "tile", None, None),
        P("edge"),
        P("edge", None),
        P("edge"),
        P("edge"),
        P(),
        P(),
        P(),
        P(),
        P(),
    )
    return jax.shard_map(
        per_device,
        mesh=mesh,
        in_specs=placed,
        out_specs=(P("edge", "tile", None, None), P("tile", "edge"), P("edge", None)),
        check_vma=False,
    )
```

profile of v0, /device:TPU:0, one launch (start us, length us, event | category | flops | bytes accessed | tf_op | source)
XLA Modules:
  0.0 204.7 jit_solution(6177645534464706526)
XLA Ops:
  7.2 0.8 fusion.173
  8.2 0.7 select_reduce_fusion.2
  8.9 0.7 fusion.198
  9.5 0.7 compare_select_fusion.4
  10.2 0.7 select_reduce_fusion
  11.0 9.7 %all_to_all.28 = s32[4,1,4]{2,1,0:T(1,128)S(1)} all-to-all(s32[4,1,4]{2,1,0:T(1,128)S(1)} %bitcast.304), channel_id=1, replica_groups=mesh['edge'=4,'tile'=8] {'edge'}, dimensions={0} | all-to-all | bytes 128 | tf_op jit(solution)/shard_map/all_to_all | solution.py:85
  21.2 0.7 reduce.106
  22.0 1.9 gather_fusion.1
  23.9 2.8 %broadcast_select_fusion = bf16[4,4,6,64,128]{4,3,2,1,0:T(8,128)(2,1)} fusion(bf16[4,4,6,64,128]{4,3,2,1,0:T(8,128)(2,1)} %bitcast.251, pred[4,4]{1,0:T(4,128)(4,1)S(1)} %compare_and_fusion), kind=kLoop, calls=%fused_computation.176 | loop fusion | flops 786432 | bytes 3145744 | tf_op jit(solution)/shard_map/jit(_take)/select_n | solution.py:88
  26.6 4.3 %all-to-all-start.1 = ((bf16[4,4,6,64,128]{4,3,2,1,0:T(8,128)(2,1)}), bf16[4,4,6,64,128]{4,3,2,1,0:T(8,128)(2,1)}, u32[]{:S(2)}, u32[]{:S(2)}) async-start(bf16[4,4,6,64,128]{4,3,2,1,0:T(8,128)(2,1)} %broadcast_select_fusion), calls=%async_computation.1 | async-start | bytes 3145728 | tf_op jit(solution)/shard_map/all_to_all | solution.py:91
  31.0 0.7 gather_fusion
  32.4 0.7 all_to_all.21
  33.7 15.4 %all-to-all-done.1 = bf16[4,4,6,64,128]{4,3,2,1,0:T(8,128)(2,1)} async-done(((bf16[4,4,6,64,128]{4,3,2,1,0:T(8,128)(2,1)}), bf16[4,4,6,64,128]{4,3,2,1,0:T(8,128)(2,1)}, u32[]{:S(2)}, u32[]{:S(2)}) %all-to-all-start.1) | async-done | bytes 1572896 | tf_op jit(solution)/shard_map/all_to_all | solution.py:91
  49.1 3.2 %all-to-all-start.2 = ((s32[4,1,4]{2,1,0:T(1,128)}), s32[4,1,4]{2,1,0:T(1,128)S(1)}, u32[]{:S(2)}, u32[]{:S(2)}) async-start(s32[4,1,4]{2,1,0:T(1,128)} %bitcast.116), calls=%async_computation.2 | async-start | bytes 4096 | tf_op jit(solution)/shard_map/all_to_all | solution.py:86
  52.4 2.1 %gather_fusion.2 = bf16[8,6,64,128]{3,2,1,0:T(8,128)(2,1)S(1)} fusion(bf16[16,6,64,128]{3,2,1,0:T(8,128)(2,1)} %bitcast.9, s32[1024]{0:T(1024)S(1)} %pad_clamp_fusion), kind=kCustom, calls=%fused_computation.2 | custom fusion | bytes 1572896 | tf_op jit(solution)/shard_map/jit(_take)/gather | solution.py:92
  54.7 1.3 collective-permute-start
  56.0 1.3 collective-permute-start.1
  57.9 0.7 reduce.107
  58.7 0.6 broadcast_subtract_fusion
  59.3 2.1 %collective-permute-done.1 = bf16[8,3,64,128]{3,2,1,0:T(8,128)(2,1)S(1)} collective-permute-done((bf16[8,3,64,128]{3,2,1,0:T(8,128)(2,1)S(1)}, bf16[8,3,64,128]{3,2,1,0:T(8,128)(2,1)S(1)}, u32[]{:S(2)}, u32[]{:S(2)}) %collective-permute-start.1) | collective-permute-done | bytes 393248 | tf_op jit(solution)/shard_map/ppermute | solution.py:21
  61.4 1.0 fusion.29
  62.4 7.7 %fusion.75 = (f32[8,6,64]{2,1,0:T(8,128)S(1)}, f32[8,6,64]{2,1,0:T(8,128)S(1)}, f32[8,6,64]{2,1,0:T(8,128)S(1)}, f32[8,6,64]{2,1,0:T(8,128)S(1)}, f32[8,6,64]{2,...) fusion(bf16[8,12,70,128]{3,2,1,0:T(8,128)(2,1)S(1)} %fusion.29,, ...), kind=kLoop, calls=%fused_computation.154 | loop fusion | flops 20788224 | bytes 14364680
  70.1 7.6 %fusion.95 = (f32[8,6,64]{2,1,0:T(8,128)S(1)}, f32[8,6,64]{2,1,0:T(8,128)S(1)}, f32[8,6,64]{2,1,0:T(8,128)S(1)}, f32[8,6,64]{2,1,0:T(8,128)S(1)}, f32[8,6,64]{2,...) fusion(bf16[8,12,70,128]{3,2,1,0:T(8,128)(2,1)S(1)} %fusion.29,, ...), kind=kLoop, calls=%fused_computation.174 | loop fusion | flops 20788224 | bytes 14364680
  77.8 3.6 %fusion.55 = (f32[8,6,64]{2,1,0:T(8,128)S(1)}, f32[8,6,64]{2,1,0:T(8,128)S(1)}, f32[8,6,64]{2,1,0:T(8,128)S(1)}, f32[8,6,64]{2,1,0:T(8,128)S(1)}, f32[8,6,64]{2,...) fusion(bf16[8,12,70,128]{3,2,1,0:T(8,128)(2,1)S(1)} %fusion.29, ...), kind=kLoop, calls=%fused_computation.134 | loop fusion | flops 10199040 | bytes 7176200
  82.0 0.6 copy.227
  82.6 0.6 copy.228
  83.2 0.6 copy.229
  84.4 0.6 copy.199
  85.0 0.6 copy.200
  85.6 0.6 copy.201
  86.2 0.6 copy.203
  86.9 0.6 copy.204
  87.5 0.6 copy.205
  88.1 0.6 copy.206
  88.7 0.6 copy.207
  89.4 3.4 %fusion.92 = (f32[8,6,64]{2,1,0:T(8,128)S(1)}, f32[8,6,64]{2,1,0:T(8,128)S(1)}, f32[8,6,64]{2,1,0:T(8,128)S(1)}, f32[8,6,64]{2,1,0:T(8,128)S(1)}, f32[8,6,64]{2,...) fusion(bf16[8,3,64,128]{3,2,1,0:T(8,128)(2,1)S(1)} %collective-permute-done.1, ...), kind=kLoop, calls=%fused_computation.171 | loop fusion | flops 11381760 | bytes 2445320
  93.0 8.1 %stack.199 = f32[8,6,64,49]{2,3,1,0:T(8,128)} concatenate(f32[8,6,64,1]{2,3,1,0:T(1,128)} %copy.199, f32[8,6,64,1]{2,3,1,0:T(1,128)} %copy.200, f32[8,6,64,1]{2,3,1,0:T(1,128)} %copy.201, f32[8,6,64,1]{2,3,1,0:T(1,128)S(1)} %copy.202, f32[8,6,64,1]{2,3,1,0:T(1,128)} %copy.203, f32[8,6,64,1]{2,3,1,0:T(1,128)} %copy.204, f32[8,6,64,1]{2,3,1,0:T(1,128)} %copy.205, ...), dimensions={3} | concatenate | bytes 1204224 | tf_op jit(solution)/shard_map/stack | solution.py:108
  101.1 1.8 maximum_convert_fusion
  103.1 8.0 %collective-permute-start.2 = (bf16[8,1,64,256]{3,2,1,0:T(8,128)(2,1)S(1)}, bf16[8,1,64,256]{3,2,1,0:T(8,128)(2,1)S(1)}, u32[]{:S(2)}, u32[]{:S(2)}) collective-permute-start(bf16[8,1,64,256]{3,2,1,0:T(8,128)(2,1)S(1)} %get-tuple-element.63), channel_id=1, source_target_pairs={{0,1},{1,2},{2,3},{3,4},{4,5},{5,6},{6,7},{8,9},{9,10},{10,11},{11... | collective-permute-start | bytes 786440 | tf_op jit(solution)/shard_map/ppermute | solution.py:19
  111.1 1.3 collective-permute-start.3
  113.0 1.5 collective-permute-done.3
  116.6 0.6 fusion.33
  117.2 0.6 fusion.34
  117.8 2.2 %fusion.15 = f32[8,6,64,256]{3,2,1,0:T(8,128)} fusion(bf16[8,6,64,128]{3,2,1,0:T(8,128)(2,1)S(1)} %maximum_convert_fusion, bf16[8,6,64,128]{3,2,1,0:T(8,128)(2,1)S(1)} %copy-done.2, bf16[8,1,64,256]{3,2,1,0:T(8,128)(2,1)S(1)} %collective-permute-done.2, bf16[3,3,256,256]{3,2,1,0:T(8,128)(2,1)S(1)} %copy-done.4), kind=kOutput, calls=%fused_computation.84 | convolution fusion | flops 408158208 | bytes 5111808 | tf_op jit(solution)/shard_map/erwc,ck->erwk/dot_general | solution.py:39
  120.0 2.3 %fusion.9 = f32[8,6,64,256]{3,2,1,0:T(8,128)} fusion(bf16[8,6,64,128]{3,2,1,0:T(8,128)(2,1)S(1)} %maximum_convert_fusion, bf16[8,1,64,256]{3,2,1,0:T(8,128)(2,1)S(1)} %collective-permute-done.3, bf16[8,6,64,128]{3,2,1,0:T(8,128)(2,1)S(1)} %copy-done.2, bf16[3,3,256,256]{3,2,1,0:T(8,128)(2,1)S(1)} %copy-done.4), kind=kOutput, calls=%fused_computation.80 | convolution fusion | flops 408158208 | bytes 5111808 | tf_op jit(solution)/shard_map/erwc,ck->erwk/dot_general | solution.py:39
  122.3 5.2 %add_divide_fusion = f32[8,6,64,256]{3,2,1,0:T(8,128)} fusion(f32[8,6,64,256]{3,2,1,0:T(8,128)} %fusion.9, f32[8,6,64,256]{3,2,1,0:T(8,128)S(1)} %fusion.34, f32[8,6,64,256]{3,2,1,0:T(8,128)S(1)} %fusion.33, f32[8,6,64,256]{3,2,1,0:T(8,128)S(1)} %fusion.45, f32[8,6,64,256]{3,2,1,0:T(8,128)S(1)} %fusion.32, f32[8,6,64,256]{3,2,1,0:T(8,128)S(1)} %fusion.31, ...), kind=kOutput, calls=%fused_computation.55 | convolution fusion | flops 411303936 | bytes 30539776 | tf_op jit(solution)/shard_map/erwc,ck->erwk/dot_general | solution.py:39
  127.5 1.7 fusion.44
  129.3 6.3 %collective-permute-start.4 = (bf16[8,1,64,256]{3,2,1,0:T(8,128)(2,1)S(1)}, bf16[8,1,64,256]{3,2,1,0:T(8,128)(2,1)S(1)}, u32[]{:S(2)}, u32[]{:S(2)}) collective-permute-start(bf16[8,1,64,256]{3,2,1,0:T(8,128)(2,1)S(1)} %get-tuple-element.61), channel_id=1, source_target_pairs={{0,1},{1,2},{2,3},{3,4},{4,5},{5,6},{6,7},{8,9},{9,10},{10,11},{11... | collective-permute-start | bytes 786440 | tf_op jit(solution)/shard_map/ppermute | solution.py:19
  135.6 1.5 collective-permute-start.5
  137.7 1.3 collective-permute-done.5
  143.4 1.3 copy-done.3
  144.7 2.3 %broadcast_select_fusion.3 = (bf16[8,6,64,128]{3,2,1,0:T(8,128)(2,1)}, bf16[8,6,64,128]{3,2,1,0:T(8,128)(2,1)S(1)}) fusion(bf16[8,6,64,128]{3,2,1,0:T(8,128)(2,1)S(1)} %copy-done.2, pred[8]{0:T(512)(128)(4,1)S(1)} %copy-done.15, bf16[3,3,256,128]{3,2,1,0:T(8,128)(2,1)S(1)} %copy-done.5, bf16[8,8,64,256]{3,2,1,0:T(8,128)(2,1)S(1)} %fusion.4, ...), kind=kOutput, calls=%fused_computation.199 | convolution fusion | flops 207224832 | bytes 18678272 | tf_op jit(solution)/shard_map/erwc,ck->erwk/dot_general | solution.py:39
  147.0 0.7 convolution_bitcast_fusion
  148.4 0.7 compare_select_fusion
  149.3 0.6 fusion.96
  150.1 0.9 fusion.166
  151.0 4.2 %all-to-all-start.3 = ((f32[4,4,72]{2,1,0:T(4,128)}), f32[4,4,72]{2,1,0:T(4,128)S(1)}, u32[]{:S(2)}, u32[]{:S(2)}) async-start(f32[4,4,72]{2,1,0:T(4,128)} %bitcast.126), calls=%async_computation.3 | async-start | bytes 16384 | tf_op jit(solution)/shard_map/all_to_all | solution.py:146
  155.5 4.4 %all-to-all-done.3 = f32[4,4,72]{2,1,0:T(4,128)S(1)} async-done(((f32[4,4,72]{2,1,0:T(4,128)}), f32[4,4,72]{2,1,0:T(4,128)S(1)}, u32[]{:S(2)}, u32[]{:S(2)}) %all-to-all-start.3) | async-done | bytes 4640 | tf_op jit(solution)/shard_map/all_to_all | solution.py:146
  160.4 1.1 convolution_convert_fusion
  161.4 1.3 copy.258
  162.7 0.9 convert_element_type.73
  163.9 28.7 %psum.7 = f32[24,36]{1,0:T(8,128)} all-reduce(f32[24,36]{1,0:T(8,128)S(1)} %fusion.148), channel_id=1, replica_groups=mesh['edge'=4,'tile'=8] {'tile'}, use_global_device_ids=true, to_apply=%region_5.6 | all-reduce | flops 864 | bytes 6912 | tf_op jit(solution)/shard_map/psum | solution.py:186
  192.6 3.9 %reduce-scatter.2.cloned.1.call-done = bf16[72,144]{1,0:T(8,128)(2,1)} async-done(((bf16[576,144]{1,0:T(8,128)(2,1)}), bf16[72,144]{1,0:T(8,128)(2,1)}) %reduce-scatter.2.cloned.1.call-update) | async-done | bytes 20752 | tf_op jit(solution)/shard_map/reduce_scatter | solution.py:180
  196.5 1.4 convert_element_type.74
  (142 shorter events, 13.1 us)
Async XLA Ops:
  7.2 14.8 %copy-start = (bf16[24,6,64,128]{3,2,1,0:T(8,128)(2,1)S(1)}, bf16[24,6,64,128]{3,2,1,0:T(8,128)(2,1)}, u32[]{:S(2)}) copy-start(bf16[24,6,64,128]{3,2,1,0:T(8,128)(2,1)} %param.11) | copy-start | bytes 7077892
  26.6 22.5 %all-to-all-start.1 = ((bf16[4,4,6,64,128]{4,3,2,1,0:T(8,128)(2,1)}), bf16[4,4,6,64,128]{4,3,2,1,0:T(8,128)(2,1)}, u32[]{:S(2)}, u32[]{:S(2)}) async-start(bf16[4,4,6,64,128]{4,3,2,1,0:T(8,128)(2,1)} %broadcast_select_fusion), calls=%async_computation.1 | async-start | bytes 3145728 | tf_op jit(solution)/shard_map/all_to_all | solution.py:91
  31.0 2.7 %copy-start.14 = (s32[8]{0:T(128)S(1)}, s32[8]{0:T(128)}, u32[]{:S(2)}) copy-start(s32[8]{0:T(128)} %param.13) | copy-start | bytes 100
  31.0 2.7 %copy-start.11 = (s32[8,1]{0,1:T(1,128)S(1)}, s32[8,1]{0,1:T(1,128)}, u32[]{:S(2)}) copy-start(s32[8,1]{0,1:T(1,128)} %param.14) | copy-start | bytes 100
  31.0 2.7 %copy-start.17 = (s32[8]{0:T(128)S(1)}, s32[8]{0:T(128)}, u32[]{:S(2)}) copy-start(s32[8]{0:T(128)} %param.15) | copy-start | bytes 100
  49.1 8.8 %all-to-all-start.2 = ((s32[4,1,4]{2,1,0:T(1,128)}), s32[4,1,4]{2,1,0:T(1,128)S(1)}, u32[]{:S(2)}, u32[]{:S(2)}) async-start(s32[4,1,4]{2,1,0:T(1,128)} %bitcast.116), calls=%async_computation.2 | async-start | bytes 4096 | tf_op jit(solution)/shard_map/all_to_all | solution.py:86
  54.7 4.6 %collective-permute-start = (bf16[8,3,64,128]{3,2,1,0:T(8,128)(2,1)S(1)}, bf16[8,3,64,128]{3,2,1,0:T(8,128)(2,1)S(1)}, u32[]{:S(2)}, u32[]{:S(2)}) collective-permute-start(bf16[8,3,64,128]{3,2,1,0:T(8,128)(2,1)S(1)} %get-tuple-element.65), channel_id=1, source_target_pairs={{0,1},{1,2},{2,3},{3,4},{4,5},{5,6},{6,7},{8,9},{9,10},{10,11},{11... | collective-permute-start | bytes 1179656 | tf_op jit(solution)/shard_map/ppermute | solution.py:19
  56.0 5.4 %collective-permute-start.1 = (bf16[8,3,64,128]{3,2,1,0:T(8,128)(2,1)S(1)}, bf16[8,3,64,128]{3,2,1,0:T(8,128)(2,1)S(1)}, u32[]{:S(2)}, u32[]{:S(2)}) collective-permute-start(bf16[8,3,64,128]{3,2,1,0:T(8,128)(2,1)S(1)} %get-tuple-element.66), channel_id=1, source_target_pairs={{1,0},{2,1},{3,2},{4,3},{5,4},{6,5},{7,6},{9,8},{10,9},{11,10},{12... | collective-permute-start | bytes 1179656 | tf_op jit(solution)/shard_map/ppermute | solution.py:21
  88.1 4.9 %copy-start.6 = (f32[8,6,64,1]{2,3,1,0:T(1,128)S(1)}, f32[8,6,64,1]{2,3,1,0:T(1,128)}, u32[]{:S(2)}) copy-start(f32[8,6,64,1]{2,3,1,0:T(1,128)} %copy.227) | copy-start | bytes 36868
  88.1 4.9 %copy-start.7 = (f32[8,6,64,1]{2,3,1,0:T(1,128)S(1)}, f32[8,6,64,1]{2,3,1,0:T(1,128)}, u32[]{:S(2)}) copy-start(f32[8,6,64,1]{2,3,1,0:T(1,128)} %copy.228) | copy-start | bytes 36868
  88.1 4.9 %copy-start.8 = (f32[8,6,64,1]{2,3,1,0:T(1,128)S(1)}, f32[8,6,64,1]{2,3,1,0:T(1,128)}, u32[]{:S(2)}) copy-start(f32[8,6,64,1]{2,3,1,0:T(1,128)} %copy.229) | copy-start | bytes 36868
  92.7 8.4 %copy-start.9 = (bf16[49,128]{1,0:T(8,128)(2,1)S(1)}, bf16[49,128]{1,0:T(8,128)(2,1)}, u32[]{:S(2)}) copy-start(bf16[49,128]{1,0:T(8,128)(2,1)} %param.17) | copy-start | bytes 37636
  101.1 1.8 copy-start.2
  103.0 9.4 %copy-start.4 = (bf16[3,3,256,256]{3,2,1,0:T(8,128)(2,1)S(1)}, bf16[3,3,256,256]{3,2,1,0:T(8,128)(2,1)}, u32[]{:S(2)}) copy-start(bf16[3,3,256,256]{3,2,1,0:T(8,128)(2,1)} %param.18) | copy-start | bytes 3538948
  103.1 9.9 %collective-permute-start.2 = (bf16[8,1,64,256]{3,2,1,0:T(8,128)(2,1)S(1)}, bf16[8,1,64,256]{3,2,1,0:T(8,128)(2,1)S(1)}, u32[]{:S(2)}, u32[]{:S(2)}) collective-permute-start(bf16[8,1,64,256]{3,2,1,0:T(8,128)(2,1)S(1)} %get-tuple-element.63), channel_id=1, source_target_pairs={{0,1},{1,2},{2,3},{3,4},{4,5},{5,6},{6,7},{8,9},{9,10},{10,11},{11... | collective-permute-start | bytes 786440 | tf_op jit(solution)/shard_map/ppermute | solution.py:19
  111.1 3.4 %collective-permute-start.3 = (bf16[8,1,64,256]{3,2,1,0:T(8,128)(2,1)S(1)}, bf16[8,1,64,256]{3,2,1,0:T(8,128)(2,1)S(1)}, u32[]{:S(2)}, u32[]{:S(2)}) collective-permute-start(bf16[8,1,64,256]{3,2,1,0:T(8,128)(2,1)S(1)} %get-tuple-element.64), channel_id=1, source_target_pairs={{1,0},{2,1},{3,2},{4,3},{5,4},{6,5},{7,6},{9,8},{10,9},{11,10},{12... | collective-permute-start | bytes 786440 | tf_op jit(solution)/shard_map/ppermute | solution.py:21
  129.2 7.9 %copy-start.5 = (bf16[3,3,256,128]{3,2,1,0:T(8,128)(2,1)S(1)}, bf16[3,3,256,128]{3,2,1,0:T(8,128)(2,1)}, u32[]{:S(2)}) copy-start(bf16[3,3,256,128]{3,2,1,0:T(8,128)(2,1)} %param.19) | copy-start | bytes 1769476
  129.3 8.4 %collective-permute-start.4 = (bf16[8,1,64,256]{3,2,1,0:T(8,128)(2,1)S(1)}, bf16[8,1,64,256]{3,2,1,0:T(8,128)(2,1)S(1)}, u32[]{:S(2)}, u32[]{:S(2)}) collective-permute-start(bf16[8,1,64,256]{3,2,1,0:T(8,128)(2,1)S(1)} %get-tuple-element.61), channel_id=1, source_target_pairs={{0,1},{1,2},{2,3},{3,4},{4,5},{5,6},{6,7},{8,9},{9,10},{10,11},{11... | collective-permute-start | bytes 786440 | tf_op jit(solution)/shard_map/ppermute | solution.py:19
  135.6 3.4 %collective-permute-start.5 = (bf16[8,1,64,256]{3,2,1,0:T(8,128)(2,1)S(1)}, bf16[8,1,64,256]{3,2,1,0:T(8,128)(2,1)S(1)}, u32[]{:S(2)}, u32[]{:S(2)}) collective-permute-start(bf16[8,1,64,256]{3,2,1,0:T(8,128)(2,1)S(1)} %get-tuple-element.62), channel_id=1, source_target_pairs={{1,0},{2,1},{3,2},{4,3},{5,4},{6,5},{7,6},{9,8},{10,9},{11,10},{12... | collective-permute-start | bytes 786440 | tf_op jit(solution)/shard_map/ppermute | solution.py:21
  142.8 1.9 copy-start.3
  142.8 1.9 copy-start.15
  144.7 2.3 %copy-start.10 = (bf16[128,24]{0,1:T(8,128)(2,1)S(1)}, bf16[128,24]{0,1:T(8,128)(2,1)}, u32[]{:S(2)}) copy-start(bf16[128,24]{0,1:T(8,128)(2,1)} %param.20) | copy-start | bytes 18436
  147.7 0.7 copy-start.19
  147.9 1.4 copy-start.16
  148.4 6.8 %copy-start.12 = (s32[48]{0:T(128)S(1)}, s32[48]{0:T(128)}, u32[]{:S(2)}) copy-start(s32[48]{0:T(128)} %get-tuple-element.59) | copy-start | bytes 580
  151.0 8.9 %all-to-all-start.3 = ((f32[4,4,72]{2,1,0:T(4,128)}), f32[4,4,72]{2,1,0:T(4,128)S(1)}, u32[]{:S(2)}, u32[]{:S(2)}) async-start(f32[4,4,72]{2,1,0:T(4,128)} %bitcast.126), calls=%async_computation.3 | async-start | bytes 16384 | tf_op jit(solution)/shard_map/all_to_all | solution.py:146
  155.2 41.3 %reduce-scatter.2.cloned.1.call-start = ((), (), s32[]{:S(2)}) async-start(), calls=%async_computation.5 | async-start | bytes 331776 | tf_op jit(solution)/shard_map/reduce_scatter | solution.py:180
  160.2 37.7 %copy-start.1 = (bf16[24,6,64,128]{3,2,1,0:T(8,128)(2,1)S(1)}, bf16[24,6,64,128]{3,2,1,0:T(8,128)(2,1)}, u32[]{:S(2)}) copy-start(bf16[24,6,64,128]{3,2,1,0:T(8,128)(2,1)} %param.11) | copy-start | bytes 7077892
  160.3 3.5 %copy-start.13 = (s32[48]{0:T(128)S(1)}, s32[48]{0:T(128)}, u32[]{:S(2)}) copy-start(s32[48]{0:T(128)} %get-tuple-element.59) | copy-start | bytes 580
  160.4 3.4 %copy-start.18 = (f32[48]{0:T(128)S(1)}, f32[48]{0:T(128)}, u32[]{:S(2)}) copy-start(f32[48]{0:T(128)} %get-tuple-element.58) | copy-start | bytes 580
Sparse Core Ops, SparseCore 0:
  163.7 32.7 reduce-scatter.1
where the time goes:
time: 206 us; the launch traced here: 205 us
  blocking collectives  38.4 us (19%)
  other arithmetic  36.9 us (18%)
  starting transfers between devices  31.5 us (15%)
  waiting for transfers between devices  28.7 us (14%)
  local copies, waits for them, and re-layouts  27.6 us (13%)
  matrix products  26.1 us (13%)
  between operations  15.6 us (8%)
    psum x1, blocking collectives, per_device(): pose_diagonal = lax.psum(diagonal_part, 'tile')  28.7 us
    unnamed x4, other arithmetic  22.3 us
    dot_general x18, matrix products, convolve(): jnp.einsum('erwc,ck->erwk', window, weight[row_step, col_step], preferred...  20.2 us
    another operation x50, local copies, waits for them, and re-layouts, per_device(): jnp.stack(columns, axis=-1) * features.shape[3] ** (-0.5)  16 us
    ppermute x3, starting transfers between devices, padded_2(): lax.ppermute(tail, axis, [(i, (i + 1) % count) for i in range(ends)])  15.7 us
    all_to_all x1, waiting for transfers between devices, per_device(): lax.all_to_all(asked, 'edge', split_axis=0, concat_axis=0, tiled=True)  15.4 us
    all_to_all x1, blocking collectives, per_device(): lax.all_to_all(send_target, 'edge', split_axis=0, concat_axis=0, tiled=True)  9.66 us
    ppermute x3, waiting for transfers between devices, padded_2(): lax.ppermute(head, axis, [((i + 1) % count, i) for i in range(ends)])  4.95 us
  transfers between devices with their start and end apart: 10, of which 6 were waited for; matrix products, arithmetic and copies ran while one was open for 4% of the time, Pallas kernels for 0%

commit v1 on v0

--- a/solution.py
+++ b/solution.py
@@ -6,6 +6,14 @@
 MAPH = 48
 MAPW = 64
 WINDOW = 7
+
+
+def doubling_sum(x, axis):
+    size, total = (lax.axis_size(axis), x)
+    for hop in [1 << k for k in range(size.bit_length() - 1)]:
+        pairs = [(i, i ^ hop) for i in range(size)]
+        total = total + lax.ppermute(total, axis, pairs)
+    return total
 
 
 def padded_2(cells, sides, width):
@@ -183,7 +191,7 @@
         scatter_dimension=0,
         tiled=True,
     ).astype(jnp.float32)
-    pose_diagonal = lax.psum(diagonal_part, "tile")
+    pose_diagonal = doubling_sum(diagonal_part, "tile")
     return (hidden_next, camera_hessian, pose_diagonal)
 
 

time: 206 us -> 206 us (level)
  blocking collectives: 38.4 us -> 9.66 us
  waiting for transfers between devices: 28.7 us -> 49.6 us
  starting transfers between devices: 31.5 us -> 38.5 us
    psum x1 -> x0, blocking collectives: 28.7 us -> none  [per_device(): pose_diagonal = lax.psum(diagonal_part, 'tile')]
    reduce_scatter x1, waiting for transfers between devices: 3.85 us -> 19.8 us  [per_device(): lax.psum_scatter(placed.reshape(own_rows * lax.axis_size('tile'), frame_t...]
    ppermute x0 -> x3, starting transfers between devices: none -> 7.05 us  [doubling_sum(): total = total + lax.ppermute(total, axis, pairs)]
    ppermute x0 -> x3, waiting for transfers between devices: none -> 4.98 us  [doubling_sum(): total = total + lax.ppermute(total, axis, pairs)]
  transfers between devices with their start and end apart: 10 -> 13, of which waited for: 6 -> 9; matrix products, arithmetic and copies ran while one was open for 4% -> 4% of each run, Pallas kernels for 0% -> 0%
where the time goes in v1:
time: 206 us; the launch traced here: 205 us
  waiting for transfers between devices  49.6 us (24%)
  starting transfers between devices  38.5 us (19%)
  other arithmetic  37.6 us (18%)
  local copies, waits for them, and re-layouts  27.6 us (13%)
  matrix products  26.1 us (13%)
  between operations  15.6 us (8%)
  blocking collectives  9.66 us (5%)
    unnamed x4, other arithmetic  22.3 us
    dot_general x18, matrix products, convolve(): jnp.einsum('erwc,ck->erwk', window, weight[row_step, col_step], preferred...  20.2 us
    reduce_scatter x1, waiting for transfers between devices, per_device(): lax.psum_scatter(placed.reshape(own_rows * lax.axis_size('tile'), frame_t...  19.8 us
    another operation x50, local copies, waits for them, and re-layouts, per_device(): jnp.stack(columns, axis=-1) * features.shape[3] ** (-0.5)  16 us
    ppermute x3, starting transfers between devices, padded_2(): lax.ppermute(tail, axis, [(i, (i + 1) % count) for i in range(ends)])  15.7 us
    all_to_all x1, waiting for transfers between devices, per_device(): lax.all_to_all(asked, 'edge', split_axis=0, concat_axis=0, tiled=True)  15.4 us
    all_to_all x1, blocking collectives, per_device(): lax.all_to_all(send_target, 'edge', split_axis=0, concat_axis=0, tiled=True)  9.66 us
    ppermute x3, starting transfers between devices, doubling_sum(): total = total + lax.ppermute(total, axis, pairs)  7.05 us
  transfers between devices with their start and end apart: 13, of which 9 were waited for; matrix products, arithmetic and copies ran while one was open for 4% of the time, Pallas kernels for 0%

profile of v1, /device:TPU:0, one launch (start us, length us, event | category | flops | bytes accessed | tf_op | source)
XLA Modules:
  0.0 204.7 jit_solution(2829787406782188017)
XLA Ops:
  7.2 0.8 fusion.173
  8.2 0.7 select_reduce_fusion.2
  8.9 0.7 fusion.198
  9.5 0.7 compare_select_fusion.4
  10.2 0.7 select_reduce_fusion
  11.0 9.7 %all_to_all.28 = s32[4,1,4]{2,1,0:T(1,128)S(1)} all-to-all(s32[4,1,4]{2,1,0:T(1,128)S(1)} %bitcast.304), channel_id=1, replica_groups=mesh['edge'=4,'tile'=8] {'edge'}, dimensions={0} | all-to-all | bytes 128 | tf_op jit(solution)/shard_map/all_to_all | solution.py:93
  21.2 0.7 reduce.106
  22.0 1.9 gather_fusion.1
  23.9 2.8 %broadcast_select_fusion = bf16[4,4,6,64,128]{4,3,2,1,0:T(8,128)(2,1)} fusion(bf16[4,4,6,64,128]{4,3,2,1,0:T(8,128)(2,1)} %bitcast.251, pred[4,4]{1,0:T(4,128)(4,1)S(1)} %compare_and_fusion), kind=kLoop, calls=%fused_computation.176 | loop fusion | flops 786432 | bytes 3145744 | tf_op jit(solution)/shard_map/jit(_take)/select_n | solution.py:96
  26.6 4.3 %all-to-all-start.1 = ((bf16[4,4,6,64,128]{4,3,2,1,0:T(8,128)(2,1)}), bf16[4,4,6,64,128]{4,3,2,1,0:T(8,128)(2,1)}, u32[]{:S(2)}, u32[]{:S(2)}) async-start(bf16[4,4,6,64,128]{4,3,2,1,0:T(8,128)(2,1)} %broadcast_select_fusion), calls=%async_computation.1 | async-start | bytes 3145728 | tf_op jit(solution)/shard_map/all_to_all | solution.py:99
  31.0 0.7 gather_fusion
  32.4 0.7 all_to_all.21
  33.7 15.4 %all-to-all-done.1 = bf16[4,4,6,64,128]{4,3,2,1,0:T(8,128)(2,1)} async-done(((bf16[4,4,6,64,128]{4,3,2,1,0:T(8,128)(2,1)}), bf16[4,4,6,64,128]{4,3,2,1,0:T(8,128)(2,1)}, u32[]{:S(2)}, u32[]{:S(2)}) %all-to-all-start.1) | async-done | bytes 1572896 | tf_op jit(solution)/shard_map/all_to_all | solution.py:99
  49.1 3.2 %all-to-all-start.2 = ((s32[4,1,4]{2,1,0:T(1,128)}), s32[4,1,4]{2,1,0:T(1,128)S(1)}, u32[]{:S(2)}, u32[]{:S(2)}) async-start(s32[4,1,4]{2,1,0:T(1,128)} %bitcast.116), calls=%async_computation.2 | async-start | bytes 4096 | tf_op jit(solution)/shard_map/all_to_all | solution.py:94
  52.4 2.1 %gather_fusion.2 = bf16[8,6,64,128]{3,2,1,0:T(8,128)(2,1)S(1)} fusion(bf16[16,6,64,128]{3,2,1,0:T(8,128)(2,1)} %bitcast.9, s32[1024]{0:T(1024)S(1)} %pad_clamp_fusion), kind=kCustom, calls=%fused_computation.2 | custom fusion | bytes 1572896 | tf_op jit(solution)/shard_map/jit(_take)/gather | solution.py:100
  54.7 1.3 collective-permute-start
  56.0 1.3 collective-permute-start.1
  57.9 0.7 reduce.107
  59.3 2.1 %collective-permute-done.1 = bf16[8,3,64,128]{3,2,1,0:T(8,128)(2,1)S(1)} collective-permute-done((bf16[8,3,64,128]{3,2,1,0:T(8,128)(2,1)S(1)}, bf16[8,3,64,128]{3,2,1,0:T(8,128)(2,1)S(1)}, u32[]{:S(2)}, u32[]{:S(2)}) %collective-permute-start.1) | collective-permute-done | bytes 393248 | tf_op jit(solution)/shard_map/ppermute | solution.py:29
  61.4 1.0 fusion.29
  62.4 7.7 %fusion.75 = (f32[8,6,64]{2,1,0:T(8,128)S(1)}, f32[8,6,64]{2,1,0:T(8,128)S(1)}, f32[8,6,64]{2,1,0:T(8,128)S(1)}, f32[8,6,64]{2,1,0:T(8,128)S(1)}, f32[8,6,64]{2,...) fusion(bf16[8,12,70,128]{3,2,1,0:T(8,128)(2,1)S(1)} %fusion.29,, ...), kind=kLoop, calls=%fused_computation.154 | loop fusion | flops 20788224 | bytes 14364680
  70.1 7.6 %fusion.95 = (f32[8,6,64]{2,1,0:T(8,128)S(1)}, f32[8,6,64]{2,1,0:T(8,128)S(1)}, f32[8,6,64]{2,1,0:T(8,128)S(1)}, f32[8,6,64]{2,1,0:T(8,128)S(1)}, f32[8,6,64]{2,...) fusion(bf16[8,12,70,128]{3,2,1,0:T(8,128)(2,1)S(1)} %fusion.29,, ...), kind=kLoop, calls=%fused_computation.174 | loop fusion | flops 20788224 | bytes 14364680
  77.8 3.6 %fusion.55 = (f32[8,6,64]{2,1,0:T(8,128)S(1)}, f32[8,6,64]{2,1,0:T(8,128)S(1)}, f32[8,6,64]{2,1,0:T(8,128)S(1)}, f32[8,6,64]{2,1,0:T(8,128)S(1)}, f32[8,6,64]{2,...) fusion(bf16[8,12,70,128]{3,2,1,0:T(8,128)(2,1)S(1)} %fusion.29, ...), kind=kLoop, calls=%fused_computation.134 | loop fusion | flops 10199040 | bytes 7176200
  82.6 0.6 copy.228
  83.2 0.6 copy.229
  84.4 0.6 copy.199
  85.0 0.6 copy.200
  85.6 0.6 copy.201
  86.2 0.6 copy.203
  86.9 0.6 copy.204
  88.1 0.6 copy.206
  88.7 0.6 copy.207
  89.4 3.4 %fusion.92 = (f32[8,6,64]{2,1,0:T(8,128)S(1)}, f32[8,6,64]{2,1,0:T(8,128)S(1)}, f32[8,6,64]{2,1,0:T(8,128)S(1)}, f32[8,6,64]{2,1,0:T(8,128)S(1)}, f32[8,6,64]{2,...) fusion(bf16[8,3,64,128]{3,2,1,0:T(8,128)(2,1)S(1)} %collective-permute-done.1, ...), kind=kLoop, calls=%fused_computation.171 | loop fusion | flops 11381760 | bytes 2445320
  93.0 8.1 %stack.199 = f32[8,6,64,49]{2,3,1,0:T(8,128)} concatenate(f32[8,6,64,1]{2,3,1,0:T(1,128)} %copy.199, f32[8,6,64,1]{2,3,1,0:T(1,128)} %copy.200, f32[8,6,64,1]{2,3,1,0:T(1,128)} %copy.201, f32[8,6,64,1]{2,3,1,0:T(1,128)S(1)} %copy.202, f32[8,6,64,1]{2,3,1,0:T(1,128)} %copy.203, f32[8,6,64,1]{2,3,1,0:T(1,128)} %copy.204, f32[8,6,64,1]{2,3,1,0:T(1,128)} %copy.205, ...), dimensions={3} | concatenate | bytes 1204224 | tf_op jit(solution)/shard_map/stack | solution.py:116
  101.1 1.8 maximum_convert_fusion
  103.1 8.0 %collective-permute-start.2 = (bf16[8,1,64,256]{3,2,1,0:T(8,128)(2,1)S(1)}, bf16[8,1,64,256]{3,2,1,0:T(8,128)(2,1)S(1)}, u32[]{:S(2)}, u32[]{:S(2)}) collective-permute-start(bf16[8,1,64,256]{3,2,1,0:T(8,128)(2,1)S(1)} %get-tuple-element.63), channel_id=1, source_target_pairs={{0,1},{1,2},{2,3},{3,4},{4,5},{5,6},{6,7},{8,9},{9,10},{10,11},{11... | collective-permute-start | bytes 786440 | tf_op jit(solution)/shard_map/ppermute | solution.py:27
  111.1 1.3 collective-permute-start.3
  113.0 1.5 collective-permute-done.3
  117.8 2.2 %fusion.15 = f32[8,6,64,256]{3,2,1,0:T(8,128)} fusion(bf16[8,6,64,128]{3,2,1,0:T(8,128)(2,1)S(1)} %maximum_convert_fusion, bf16[8,6,64,128]{3,2,1,0:T(8,128)(2,1)S(1)} %copy-done.2, bf16[8,1,64,256]{3,2,1,0:T(8,128)(2,1)S(1)} %collective-permute-done.2, bf16[3,3,256,256]{3,2,1,0:T(8,128)(2,1)S(1)} %copy-done.4), kind=kOutput, calls=%fused_computation.84 | convolution fusion | flops 408158208 | bytes 5111808 | tf_op jit(solution)/shard_map/erwc,ck->erwk/dot_general | solution.py:47
  120.0 2.3 %fusion.9 = f32[8,6,64,256]{3,2,1,0:T(8,128)} fusion(bf16[8,6,64,128]{3,2,1,0:T(8,128)(2,1)S(1)} %maximum_convert_fusion, bf16[8,1,64,256]{3,2,1,0:T(8,128)(2,1)S(1)} %collective-permute-done.3, bf16[8,6,64,128]{3,2,1,0:T(8,128)(2,1)S(1)} %copy-done.2, bf16[3,3,256,256]{3,2,1,0:T(8,128)(2,1)S(1)} %copy-done.4), kind=kOutput, calls=%fused_computation.80 | convolution fusion | flops 408158208 | bytes 5111808 | tf_op jit(solution)/shard_map/erwc,ck->erwk/dot_general | solution.py:47
  122.3 5.2 %add_divide_fusion = f32[8,6,64,256]{3,2,1,0:T(8,128)} fusion(f32[8,6,64,256]{3,2,1,0:T(8,128)} %fusion.9, f32[8,6,64,256]{3,2,1,0:T(8,128)S(1)} %fusion.34, f32[8,6,64,256]{3,2,1,0:T(8,128)S(1)} %fusion.33, f32[8,6,64,256]{3,2,1,0:T(8,128)S(1)} %fusion.45, f32[8,6,64,256]{3,2,1,0:T(8,128)S(1)} %fusion.32, f32[8,6,64,256]{3,2,1,0:T(8,128)S(1)} %fusion.31, ...), kind=kOutput, calls=%fused_computation.55 | convolution fusion | flops 411303936 | bytes 30539776 | tf_op jit(solution)/shard_map/erwc,ck->erwk/dot_general | solution.py:47
  127.5 1.7 fusion.44
  129.3 6.3 %collective-permute-start.4 = (bf16[8,1,64,256]{3,2,1,0:T(8,128)(2,1)S(1)}, bf16[8,1,64,256]{3,2,1,0:T(8,128)(2,1)S(1)}, u32[]{:S(2)}, u32[]{:S(2)}) collective-permute-start(bf16[8,1,64,256]{3,2,1,0:T(8,128)(2,1)S(1)} %get-tuple-element.61), channel_id=1, source_target_pairs={{0,1},{1,2},{2,3},{3,4},{4,5},{5,6},{6,7},{8,9},{9,10},{10,11},{11... | collective-permute-start | bytes 786440 | tf_op jit(solution)/shard_map/ppermute | solution.py:27
  135.6 1.5 collective-permute-start.5
  137.7 1.3 collective-permute-done.5
  143.4 1.3 copy-done.3
  144.7 2.3 %broadcast_select_fusion.3 = (bf16[8,6,64,128]{3,2,1,0:T(8,128)(2,1)}, bf16[8,6,64,128]{3,2,1,0:T(8,128)(2,1)S(1)}) fusion(bf16[8,6,64,128]{3,2,1,0:T(8,128)(2,1)S(1)} %copy-done.2, pred[8]{0:T(512)(128)(4,1)S(1)} %copy-done.15, bf16[3,3,256,128]{3,2,1,0:T(8,128)(2,1)S(1)} %copy-done.5, bf16[8,8,64,256]{3,2,1,0:T(8,128)(2,1)S(1)} %fusion.4, ...), kind=kOutput, calls=%fused_computation.199 | convolution fusion | flops 207224832 | bytes 18678272 | tf_op jit(solution)/shard_map/erwc,ck->erwk/dot_general | solution.py:47
  147.0 0.7 convolution_bitcast_fusion
  148.4 0.7 compare_select_fusion
  149.3 0.6 fusion.96
  150.1 0.9 fusion.166
  151.0 4.2 %all-to-all-start.3 = ((f32[4,4,72]{2,1,0:T(4,128)}), f32[4,4,72]{2,1,0:T(4,128)S(1)}, u32[]{:S(2)}, u32[]{:S(2)}) async-start(f32[4,4,72]{2,1,0:T(4,128)} %bitcast.126), calls=%async_computation.3 | async-start | bytes 16384 | tf_op jit(solution)/shard_map/all_to_all | solution.py:154
  155.5 4.4 %all-to-all-done.3 = f32[4,4,72]{2,1,0:T(4,128)S(1)} async-done(((f32[4,4,72]{2,1,0:T(4,128)}), f32[4,4,72]{2,1,0:T(4,128)S(1)}, u32[]{:S(2)}, u32[]{:S(2)}) %all-to-all-start.3) | async-done | bytes 4640 | tf_op jit(solution)/shard_map/all_to_all | solution.py:154
  160.4 1.1 convolution_convert_fusion
  161.4 1.3 copy.258
  162.7 0.9 convert_element_type.73
  163.9 2.9 %collective-permute-start.6 = (f32[24,36]{1,0:T(8,128)S(1)}, f32[24,36]{1,0:T(8,128)S(1)}, u32[]{:S(2)}, u32[]{:S(2)}) collective-permute-start(f32[24,36]{1,0:T(8,128)S(1)} %fusion.148), channel_id=1, source_target_pairs={{0,1},{1,0},{2,3},{3,2},{4,5},{5,4},{6,7},{7,6},{8,9},{9,8},{10,11... | collective-permute-start | bytes 10376 | tf_op jit(solution)/shard_map/ppermute | solution.py:15
  166.8 0.8 collective-permute-done.6
  167.7 1.6 collective-permute-start.7
  169.2 2.1 %collective-permute-done.7 = f32[24,36]{1,0:T(8,128)S(1)} collective-permute-done((f32[24,36]{1,0:T(8,128)S(1)}, f32[24,36]{1,0:T(8,128)S(1)}, u32[]{:S(2)}, u32[]{:S(2)}) %collective-permute-start.7) | collective-permute-done | bytes 3488 | tf_op jit(solution)/shard_map/ppermute | solution.py:15
  171.4 2.6 %collective-permute-start.8 = (f32[24,36]{1,0:T(8,128)S(1)}, f32[24,36]{1,0:T(8,128)S(1)}, u32[]{:S(2)}, u32[]{:S(2)}) collective-permute-start(f32[24,36]{1,0:T(8,128)S(1)} %add.172), channel_id=1, source_target_pairs={{0,4},{1,5},{2,6},{3,7},{4,0},{5,1},{6,2},{7,3},{8,12},{9,13},{10,... | collective-permute-start | bytes 10376 | tf_op jit(solution)/shard_map/ppermute | solution.py:15
  173.9 2.0 collective-permute-done.8
  176.6 19.8 %reduce-scatter.2.cloned.1.call-done = bf16[72,144]{1,0:T(8,128)(2,1)} async-done(((bf16[576,144]{1,0:T(8,128)(2,1)}), bf16[72,144]{1,0:T(8,128)(2,1)}) %reduce-scatter.2.cloned.1.call-update) | async-done | bytes 20752 | tf_op jit(solution)/shard_map/reduce_scatter | solution.py:188
  196.4 1.4 convert_element_type.74
  (150 shorter events, 16.8 us)
Async XLA Ops:
  7.2 14.8 %copy-start = (bf16[24,6,64,128]{3,2,1,0:T(8,128)(2,1)S(1)}, bf16[24,6,64,128]{3,2,1,0:T(8,128)(2,1)}, u32[]{:S(2)}) copy-start(bf16[24,6,64,128]{3,2,1,0:T(8,128)(2,1)} %param.11) | copy-start | bytes 7077892
  26.6 22.5 %all-to-all-start.1 = ((bf16[4,4,6,64,128]{4,3,2,1,0:T(8,128)(2,1)}), bf16[4,4,6,64,128]{4,3,2,1,0:T(8,128)(2,1)}, u32[]{:S(2)}, u32[]{:S(2)}) async-start(bf16[4,4,6,64,128]{4,3,2,1,0:T(8,128)(2,1)} %broadcast_select_fusion), calls=%async_computation.1 | async-start | bytes 3145728 | tf_op jit(solution)/shard_map/all_to_all | solution.py:99
  31.0 2.7 %copy-start.14 = (s32[8]{0:T(128)S(1)}, s32[8]{0:T(128)}, u32[]{:S(2)}) copy-start(s32[8]{0:T(128)} %param.13) | copy-start | bytes 100
  31.0 2.7 %copy-start.11 = (s32[8,1]{0,1:T(1,128)S(1)}, s32[8,1]{0,1:T(1,128)}, u32[]{:S(2)}) copy-start(s32[8,1]{0,1:T(1,128)} %param.14) | copy-start | bytes 100
  31.0 2.7 %copy-start.17 = (s32[8]{0:T(128)S(1)}, s32[8]{0:T(128)}, u32[]{:S(2)}) copy-start(s32[8]{0:T(128)} %param.15) | copy-start | bytes 100
  49.1 8.8 %all-to-all-start.2 = ((s32[4,1,4]{2,1,0:T(1,128)}), s32[4,1,4]{2,1,0:T(1,128)S(1)}, u32[]{:S(2)}, u32[]{:S(2)}) async-start(s32[4,1,4]{2,1,0:T(1,128)} %bitcast.116), calls=%async_computation.2 | async-start | bytes 4096 | tf_op jit(solution)/shard_map/all_to_all | solution.py:94
  54.7 4.6 %collective-permute-start = (bf16[8,3,64,128]{3,2,1,0:T(8,128)(2,1)S(1)}, bf16[8,3,64,128]{3,2,1,0:T(8,128)(2,1)S(1)}, u32[]{:S(2)}, u32[]{:S(2)}) collective-permute-start(bf16[8,3,64,128]{3,2,1,0:T(8,128)(2,1)S(1)} %get-tuple-element.65), channel_id=1, source_target_pairs={{0,1},{1,2},{2,3},{3,4},{4,5},{5,6},{6,7},{8,9},{9,10},{10,11},{11... | collective-permute-start | bytes 1179656 | tf_op jit(solution)/shard_map/ppermute | solution.py:27
  56.0 5.4 %collective-permute-start.1 = (bf16[8,3,64,128]{3,2,1,0:T(8,128)(2,1)S(1)}, bf16[8,3,64,128]{3,2,1,0:T(8,128)(2,1)S(1)}, u32[]{:S(2)}, u32[]{:S(2)}) collective-permute-start(bf16[8,3,64,128]{3,2,1,0:T(8,128)(2,1)S(1)} %get-tuple-element.66), channel_id=1, source_target_pairs={{1,0},{2,1},{3,2},{4,3},{5,4},{6,5},{7,6},{9,8},{10,9},{11,10},{12... | collective-permute-start | bytes 1179656 | tf_op jit(solution)/shard_map/ppermute | solution.py:29
  88.1 4.9 %copy-start.6 = (f32[8,6,64,1]{2,3,1,0:T(1,128)S(1)}, f32[8,6,64,1]{2,3,1,0:T(1,128)}, u32[]{:S(2)}) copy-start(f32[8,6,64,1]{2,3,1,0:T(1,128)} %copy.227) | copy-start | bytes 36868
  88.1 4.9 %copy-start.7 = (f32[8,6,64,1]{2,3,1,0:T(1,128)S(1)}, f32[8,6,64,1]{2,3,1,0:T(1,128)}, u32[]{:S(2)}) copy-start(f32[8,6,64,1]{2,3,1,0:T(1,128)} %copy.228) | copy-start | bytes 36868
  88.1 4.9 %copy-start.8 = (f32[8,6,64,1]{2,3,1,0:T(1,128)S(1)}, f32[8,6,64,1]{2,3,1,0:T(1,128)}, u32[]{:S(2)}) copy-start(f32[8,6,64,1]{2,3,1,0:T(1,128)} %copy.229) | copy-start | bytes 36868
  92.7 8.4 %copy-start.9 = (bf16[49,128]{1,0:T(8,128)(2,1)S(1)}, bf16[49,128]{1,0:T(8,128)(2,1)}, u32[]{:S(2)}) copy-start(bf16[49,128]{1,0:T(8,128)(2,1)} %param.17) | copy-start | bytes 37636
  101.1 1.8 copy-start.2
  103.0 9.4 %copy-start.4 = (bf16[3,3,256,256]{3,2,1,0:T(8,128)(2,1)S(1)}, bf16[3,3,256,256]{3,2,1,0:T(8,128)(2,1)}, u32[]{:S(2)}) copy-start(bf16[3,3,256,256]{3,2,1,0:T(8,128)(2,1)} %param.18) | copy-start | bytes 3538948
  103.1 9.9 %collective-permute-start.2 = (bf16[8,1,64,256]{3,2,1,0:T(8,128)(2,1)S(1)}, bf16[8,1,64,256]{3,2,1,0:T(8,128)(2,1)S(1)}, u32[]{:S(2)}, u32[]{:S(2)}) collective-permute-start(bf16[8,1,64,256]{3,2,1,0:T(8,128)(2,1)S(1)} %get-tuple-element.63), channel_id=1, source_target_pairs={{0,1},{1,2},{2,3},{3,4},{4,5},{5,6},{6,7},{8,9},{9,10},{10,11},{11... | collective-permute-start | bytes 786440 | tf_op jit(solution)/shard_map/ppermute | solution.py:27
  111.1 3.4 %collective-permute-start.3 = (bf16[8,1,64,256]{3,2,1,0:T(8,128)(2,1)S(1)}, bf16[8,1,64,256]{3,2,1,0:T(8,128)(2,1)S(1)}, u32[]{:S(2)}, u32[]{:S(2)}) collective-permute-start(bf16[8,1,64,256]{3,2,1,0:T(8,128)(2,1)S(1)} %get-tuple-element.64), channel_id=1, source_target_pairs={{1,0},{2,1},{3,2},{4,3},{5,4},{6,5},{7,6},{9,8},{10,9},{11,10},{12... | collective-permute-start | bytes 786440 | tf_op jit(solution)/shard_map/ppermute | solution.py:29
  129.2 7.9 %copy-start.5 = (bf16[3,3,256,128]{3,2,1,0:T(8,128)(2,1)S(1)}, bf16[3,3,256,128]{3,2,1,0:T(8,128)(2,1)}, u32[]{:S(2)}) copy-start(bf16[3,3,256,128]{3,2,1,0:T(8,128)(2,1)} %param.19) | copy-start | bytes 1769476
  129.3 8.4 %collective-permute-start.4 = (bf16[8,1,64,256]{3,2,1,0:T(8,128)(2,1)S(1)}, bf16[8,1,64,256]{3,2,1,0:T(8,128)(2,1)S(1)}, u32[]{:S(2)}, u32[]{:S(2)}) collective-permute-start(bf16[8,1,64,256]{3,2,1,0:T(8,128)(2,1)S(1)} %get-tuple-element.61), channel_id=1, source_target_pairs={{0,1},{1,2},{2,3},{3,4},{4,5},{5,6},{6,7},{8,9},{9,10},{10,11},{11... | collective-permute-start | bytes 786440 | tf_op jit(solution)/shard_map/ppermute | solution.py:27
  135.6 3.4 %collective-permute-start.5 = (bf16[8,1,64,256]{3,2,1,0:T(8,128)(2,1)S(1)}, bf16[8,1,64,256]{3,2,1,0:T(8,128)(2,1)S(1)}, u32[]{:S(2)}, u32[]{:S(2)}) collective-permute-start(bf16[8,1,64,256]{3,2,1,0:T(8,128)(2,1)S(1)} %get-tuple-element.62), channel_id=1, source_target_pairs={{1,0},{2,1},{3,2},{4,3},{5,4},{6,5},{7,6},{9,8},{10,9},{11,10},{12... | collective-permute-start | bytes 786440 | tf_op jit(solution)/shard_map/ppermute | solution.py:29
  142.8 1.9 copy-start.3
  142.8 1.9 copy-start.15
  144.7 2.3 %copy-start.10 = (bf16[128,24]{0,1:T(8,128)(2,1)S(1)}, bf16[128,24]{0,1:T(8,128)(2,1)}, u32[]{:S(2)}) copy-start(bf16[128,24]{0,1:T(8,128)(2,1)} %param.20) | copy-start | bytes 18436
  147.7 0.7 copy-start.19
  147.9 1.4 copy-start.16
  148.4 6.8 %copy-start.12 = (s32[48]{0:T(128)S(1)}, s32[48]{0:T(128)}, u32[]{:S(2)}) copy-start(s32[48]{0:T(128)} %get-tuple-element.59) | copy-start | bytes 580
  151.0 8.9 %all-to-all-start.3 = ((f32[4,4,72]{2,1,0:T(4,128)}), f32[4,4,72]{2,1,0:T(4,128)S(1)}, u32[]{:S(2)}, u32[]{:S(2)}) async-start(f32[4,4,72]{2,1,0:T(4,128)} %bitcast.126), calls=%async_computation.3 | async-start | bytes 16384 | tf_op jit(solution)/shard_map/all_to_all | solution.py:154
  155.2 41.2 %reduce-scatter.2.cloned.1.call-start = ((), (), s32[]{:S(2)}) async-start(), calls=%async_computation.5 | async-start | bytes 331776 | tf_op jit(solution)/shard_map/reduce_scatter | solution.py:188
  160.3 3.5 %copy-start.13 = (s32[48]{0:T(128)S(1)}, s32[48]{0:T(128)}, u32[]{:S(2)}) copy-start(s32[48]{0:T(128)} %get-tuple-element.59) | copy-start | bytes 580
  160.3 37.5 %copy-start.1 = (bf16[24,6,64,128]{3,2,1,0:T(8,128)(2,1)S(1)}, bf16[24,6,64,128]{3,2,1,0:T(8,128)(2,1)}, u32[]{:S(2)}) copy-start(bf16[24,6,64,128]{3,2,1,0:T(8,128)(2,1)} %param.11) | copy-start | bytes 7077892
  160.4 3.4 %copy-start.18 = (f32[48]{0:T(128)S(1)}, f32[48]{0:T(128)}, u32[]{:S(2)}) copy-start(f32[48]{0:T(128)} %get-tuple-element.58) | copy-start | bytes 580
  163.9 3.7 %collective-permute-start.6 = (f32[24,36]{1,0:T(8,128)S(1)}, f32[24,36]{1,0:T(8,128)S(1)}, u32[]{:S(2)}, u32[]{:S(2)}) collective-permute-start(f32[24,36]{1,0:T(8,128)S(1)} %fusion.148), channel_id=1, source_target_pairs={{0,1},{1,0},{2,3},{3,2},{4,5},{5,4},{6,7},{7,6},{8,9},{9,8},{10,11... | collective-permute-start | bytes 10376 | tf_op jit(solution)/shard_map/ppermute | solution.py:15
  167.7 3.7 %collective-permute-start.7 = (f32[24,36]{1,0:T(8,128)S(1)}, f32[24,36]{1,0:T(8,128)S(1)}, u32[]{:S(2)}, u32[]{:S(2)}) collective-permute-start(f32[24,36]{1,0:T(8,128)S(1)} %add.171), channel_id=1, source_target_pairs={{0,2},{1,3},{2,0},{3,1},{4,6},{5,7},{6,4},{7,5},{8,10},{9,11},{10,... | collective-permute-start | bytes 10376 | tf_op jit(solution)/shard_map/ppermute | solution.py:15
  171.4 4.6 %collective-permute-start.8 = (f32[24,36]{1,0:T(8,128)S(1)}, f32[24,36]{1,0:T(8,128)S(1)}, u32[]{:S(2)}, u32[]{:S(2)}) collective-permute-start(f32[24,36]{1,0:T(8,128)S(1)} %add.172), channel_id=1, source_target_pairs={{0,4},{1,5},{2,6},{3,7},{4,0},{5,1},{6,2},{7,3},{8,12},{9,13},{10,... | collective-permute-start | bytes 10376 | tf_op jit(solution)/shard_map/ppermute | solution.py:15
Sparse Core Ops, SparseCore 0:
  163.7 32.6 reduce-scatter.1
